TPU v7x, 512 devices: a whole 4x8x8 slice. The times are simulated.
512 devices in a mesh: src: 128 (over y, z, core), depth: 4 (over x).
Axes of the slice: x: 4, y: 8, z: 8, core: 2. Of those that a mesh axis runs over, the one named last changes fastest.
Arguments:
- incident: float32 [128, 4, 2, 4096], P('src'), may hold values from -6 to 6
- encode: int32 [128], P('src'), may hold values from 0 to 15
- freq_index: int32 [128], P('src'), may hold values from 0 to 7
- wavenum: float32 [8], replicated, may hold values from 1 to 2.8
- slowness: float32 [4, 4096], P('depth'), may hold values from -6 to 6
- probes: bfloat16 [64, 4, 4096], P(None, 'depth'), may hold values from -6 to 6
Outputs:
- sketch_basis: float32 [64, 4, 4096], P(None, 'depth', 'src')
- r_factor: float32 [64, 64], replicated
All inputs are finite; a program needn't handle non-finite values.
Results may differ from a plain program's by a relative error of at most 0.02.
Values may be sent and summed in bfloat16 or wider, within the bound.
A program may use at most 128 MiB of HBM per device.

v0:
```python
import math

import jax
import jax.numpy as jnp
from jax import lax
from jax.sharding import PartitionSpec as P

SIDE = 64


DAMPING = 0.5
STEP_DEPTH = 1.0


def from_behind(x, axis, by):
    size = lax.axis_size(axis)
    pairs = [(i, i + by) for i in range(size) if 0 <= i + by < size]
    return lax.ppermute(x, axis, pairs)


def dft_tables(points, direction):
    counter = jnp.arange(points, dtype=jnp.int32)
    product = counter[:, None] * counter[None, :] % points
    angles = 2.0 * math.pi / points * product.astype(jnp.float32)
    cosine = jnp.cos(angles) / math.sqrt(points)
    sine_part = direction * jnp.sin(angles) / math.sqrt(points)
    matrix = jnp.stack(
        [jnp.stack([cosine, sine_part], axis=1), jnp.stack([-sine_part, cosine], axis=1)], axis=0
    )
    matrix = matrix.astype(jnp.bfloat16)
    total_points = points * points
    twist_index = counter[:, None] * counter[None, :] % total_points
    twist_angle = 2.0 * math.pi / total_points * twist_index.astype(jnp.float32)
    return (matrix, jnp.cos(twist_angle), direction * jnp.sin(twist_angle))


def transform(values, tables):
    matrix, twist_real, twist_imag = tables
    points = matrix.shape[1]
    leading = values.shape[:-2]
    grid_values = values.reshape((-1, 2 * points, points))
    square = matrix.reshape(2 * points, 2 * points)
    segmented = jnp.einsum("nkb,km->nbm", grid_values, square, preferred_element_type=jnp.float32)
    real_part = segmented[:, :, :points]
    imag_part = segmented[:, :, points:]
    turned = jnp.concatenate(
        [
            real_part * twist_real - imag_part * twist_imag,
            real_part * twist_imag + imag_part * twist_real,
        ],
        axis=-1,
    )
    turned = turned.astype(jnp.bfloat16).reshape((-1, points, 2, points))
    result = jnp.einsum("nbsc,sbtd->ntdc", turned, matrix, preferred_element_type=jnp.float32)
    return result.reshape(leading + (2, points * points))


def complex_times(first, second):
    real_part = first[..., 0, :] * second[..., 0, :] - first[..., 1, :] * second[..., 1, :]
    imag_part = first[..., 0, :] * second[..., 1, :] + first[..., 1, :] * second[..., 0, :]
    return jnp.stack([real_part, imag_part], axis=-2)


def conjugate(values):
    return jnp.stack([values[..., 0, :], -values[..., 1, :]], axis=-2)


def propagate(values, spectrum, forward, inverse):
    moved_on = transform(values.astype(jnp.bfloat16), forward)
    return transform(complex_times(moved_on, spectrum).astype(jnp.bfloat16), inverse)


def propagator(wave_nums, points_all):
    counter = jnp.arange(points_all, dtype=jnp.int32)
    folded = jnp.where(counter < points_all // 2, counter, counter - points_all).astype(jnp.float32)
    lateral = 2.0 * math.pi / points_all * folded
    excess = wave_nums[:, None] ** 2 - lateral[None, :] ** 2
    upward = jnp.sqrt(jnp.maximum(excess, 0.0)) * STEP_DEPTH
    damped = jnp.sqrt(jnp.maximum(-excess, 0.0)) * STEP_DEPTH
    real_part = jnp.where(excess > 0, jnp.cos(upward), jnp.exp(-damped))
    imag_part = jnp.where(excess > 0, jnp.sin(upward), jnp.zeros_like(upward))
    return jnp.stack([real_part, imag_part], axis=1)


def screens(wave_nums, slowness):
    phase = wave_nums[:, None, None] * STEP_DEPTH * slowness[None]
    return jnp.stack([jnp.cos(phase), jnp.sin(phase)], axis=2)


def encoded_sources(incident, encode, sources):
    shifts = jnp.arange(sources, dtype=jnp.int32)
    bit_set = encode[:, None] >> shifts[None, :] & 1
    signs_all = (1 - 2 * bit_set).astype(jnp.float32)
    return jnp.sum(signs_all[:, :, None, None] * incident, axis=1)


def lookup_waves(freq_index, wavenum, table_size):
    onehot_rows = (freq_index[:, None] == jnp.arange(table_size, dtype=jnp.int32)[None, :]).astype(
        jnp.float32
    )
    return jnp.sum(onehot_rows * wavenum[None, :], axis=1)


def shards(incident, encode, freq_index, wavenum, slowness, probes):
    points_all = SIDE * SIDE
    forward = dft_tables(SIDE, -1.0)
    inverse = dft_tables(SIDE, 1.0)
    group_count = incident.shape[0]
    plane_count = slowness.shape[0]
    probe_count = probes.shape[0]
    sources = encoded_sources(incident, encode, incident.shape[1])
    wave_nums = lookup_waves(freq_index, wavenum, wavenum.shape[0])
    spectra = propagator(wave_nums, points_all)
    spectra_back = conjugate(spectra)
    plane_screens = screens(wave_nums, slowness)
    born_scale = wave_nums * STEP_DEPTH
    depth_index = lax.axis_index("depth")
    depth_count = lax.axis_size("depth")

    def march_background(upper):
        current = upper
        current = complex_times(plane_screens[:, 0], propagate(current, spectra, forward, inverse))
        states = [current]
        return states

    source_low = sources.astype(jnp.bfloat16)
    received = jnp.zeros_like(source_low)
    for segment in range(depth_count - 1):
        upper = jnp.where(depth_index == 0, source_low, received)
        passing = march_background(upper)
        received = from_behind(passing[-1].astype(jnp.bfloat16), "depth", 1)
    backgrounds = march_background(jnp.where(depth_index == 0, source_low, received))

    def march_tangent(upper, probe_block):
        current = upper
        moved_on = complex_times(
            plane_screens[:, 0][:, None], propagate(current, spectra[:, None], forward, inverse)
        )
        background = backgrounds[0]
        scaled = born_scale[:, None, None] * probe_block[:, 0].astype(jnp.float32)[None]
        born_term = jnp.stack(
            [-scaled * background[:, None, 1], scaled * background[:, None, 0]], axis=2
        )
        current = moved_on + born_term
        return current

    def march_adjoint(lowest_field):
        adjoint = lowest_field
        pieces = [None] * plane_count
        for plane in reversed(range(plane_count)):
            background = backgrounds[plane]
            product_terms = born_scale[:, None, None] * (
                background[:, None, 0] * adjoint[:, :, 1]
                - background[:, None, 1] * adjoint[:, :, 0]
            )
            pieces[plane] = jnp.sum(product_terms, axis=0)
            turned_back = complex_times(conjugate(plane_screens[:, plane])[:, None], adjoint)
            adjoint = propagate(turned_back, spectra_back[:, None], forward, inverse)
        return (adjoint, jnp.stack(pieces, axis=1))

    block_rows = 4
    block_count = probe_count // block_rows
    segment_count = depth_count + block_count - 1
    field_shape = (group_count, block_rows, 2, points_all)
    received_tangent = jnp.zeros(field_shape, jnp.bfloat16)
    bottoms = jnp.zeros((group_count, probe_count + block_rows, 2, points_all), jnp.float32)
    for segment in range(segment_count):
        position = segment - depth_index
        active = (position >= 0) & (position < block_count)
        chosen = jnp.clip(position, 0, block_count - 1)
        slot = jnp.where(active, chosen * block_rows, probe_count)
        probe_block = lax.dynamic_slice_in_dim(probes, chosen * block_rows, block_rows, 0)
        upper = jnp.where(depth_index == 0, jnp.zeros_like(received_tangent), received_tangent)
        lowest = lax.cond(
            active,
            lambda: march_tangent(upper, probe_block),
            lambda: jnp.zeros(field_shape, jnp.float32),
        )
        bottoms = lax.dynamic_update_slice_in_dim(bottoms, lowest, slot, 1)
        if segment + 1 < segment_count:
            received_tangent = from_behind(lowest.astype(jnp.bfloat16), "depth", 1)
    rank_up = depth_count - 1 - depth_index
    received_adjoint = jnp.zeros(field_shape, jnp.float32)
    sketch_part = jnp.zeros((probe_count + block_rows, plane_count, points_all), jnp.float32)
    for segment in range(segment_count):
        position = segment - rank_up
        active = (position >= 0) & (position < block_count)
        chosen = jnp.clip(position, 0, block_count - 1)
        slot = jnp.where(active, chosen * block_rows, probe_count)
        seeded = lax.dynamic_slice_in_dim(bottoms, chosen * block_rows, block_rows, 1)
        lower_field = jnp.where(depth_index == depth_count - 1, seeded, received_adjoint)
        topmost, block_sketch = lax.cond(
            active,
            lambda: march_adjoint(lower_field),
            lambda: (
                jnp.zeros(field_shape, jnp.float32),
                jnp.zeros((block_rows, plane_count, points_all), jnp.float32),
            ),
        )
        sketch_part = lax.dynamic_update_slice_in_dim(sketch_part, block_sketch, slot, 0)
        if segment + 1 < segment_count:
            received_adjoint = from_behind(topmost.astype(jnp.bfloat16), "depth", -1).astype(
                topmost.dtype
            )
    summed = lax.psum_scatter(sketch_part[:probe_count], "src", scatter_dimension=2, tiled=True)
    src_count = lax.axis_size("src")
    slab_width = summed.shape[2]
    local_probes = lax.dynamic_slice_in_dim(
        probes, lax.axis_index("src") * slab_width, slab_width, 2
    ).astype(jnp.float32)
    sketch = summed / (group_count * src_count) + DAMPING * local_probes
    flattened = sketch.reshape(probe_count, plane_count * slab_width)
    row_total = plane_count * slab_width * src_count * depth_count
    gram_local = jnp.dot(flattened, flattened.T, precision=lax.Precision.HIGHEST) / row_total
    gram_matrix = lax.psum(gram_local, ("src", "depth"))
    lower_factor = jnp.linalg.cholesky(gram_matrix)
    identity = jnp.eye(probe_count, dtype=jnp.float32)
    inverse_lower = lax.linalg.triangular_solve(lower_factor, identity, left_side=True, lower=True)
    sketch_basis = jnp.dot(inverse_lower, flattened, precision=lax.Precision.HIGHEST).reshape(
        probe_count, plane_count, slab_width
    )
    return (sketch_basis, lower_factor.T)


def solution(mesh):
    in_specs = (
        P("src", None, None, None),
        P("src"),
        P("src"),
        P(),
        P("depth", None),
        P(None, "depth", None),
    )
    out_specs = (P(None, "depth", "src"), P())
    return jax.shard_map(shards, mesh=mesh, in_specs=in_specs, out_specs=out_specs, check_vma=False)
```

profile of v0, /device:TPU:1, one launch (start us, length us, event | category | flops | bytes accessed | tf_op | source)
XLA Modules:
  0.0 747.9 jit_solution(17268058572091044971)
XLA Ops:
  16.9 3.9 collective-permute-start
  38.6 4.6 conditional.38
  47.1 4.5 conditional.39
  56.7 4.5 conditional.40
  61.3 3.7 collective-permute-start.5
  66.3 4.5 conditional.41
  76.5 4.5 conditional.42
  81.1 4.0 collective-permute-start.7
  86.5 4.5 conditional.43
  91.1 4.1 collective-permute-start.8
  96.1 4.5 conditional.44
  100.7 3.7 collective-permute-start.9
  105.7 4.5 conditional.45
  115.3 4.5 conditional.46
  119.9 3.7 collective-permute-start.11
  124.9 4.5 conditional.47
  134.5 4.5 conditional.48
  139.1 3.9 collective-permute-start.13
  144.1 4.5 conditional.49
  153.7 4.5 conditional.50
  163.4 4.5 conditional.51
  173.2 4.4 conditional.52
  177.7 4.2 collective-permute-start.17
  183.2 4.4 conditional.53
  193.1 8.1 %collective-permute-start.19 = (bf16[1,4,2,4096]{3,2,1,0:T(2,128)(2,1)S(1)}, bf16[1,4,2,4096]{3,2,1,0:T(2,128)(2,1)S(1)}, u32[]{:S(2)}, u32[]{:S(2)}) collective-permute-start(bf16[1,4,2,4096]{3,2,1,0:T(2,128)(2,1)S(1)} %get-tuple-element.7639), channel_id=1, source_target_pairs={{0,1},{1,2},{2,3},{4,5},{5,6},{6,7},{8,9},{9,10},{10,11},{12,13},{... | collective-permute-start | bytes 196616 | tf_op jit(solution)/shard_map/ppermute | solution.py:18
  209.3 7.0 collective-permute-done.21
  224.6 17.3 %collective-permute-done.23 = bf16[1,4,2,4096]{3,2,1,0:T(2,128)(2,1)S(1)} collective-permute-done((bf16[1,4,2,4096]{3,2,1,0:T(2,128)(2,1)S(1)}, bf16[1,4,2,4096]{3,2,1,0:T(2,128)(2,1)S(1)}, u32[]{:S(2)}, u32[]{:S(2)}) %collective-permute-start.23) | collective-permute-done | bytes 65568 | tf_op jit(solution)/shard_map/ppermute | solution.py:18
  241.9 3.9 conditional.60
  250.9 3.9 conditional.61
  259.9 3.9 conditional.62
  269.1 3.9 conditional.63
  278.4 3.9 conditional.64
  287.5 3.9 conditional.65
  296.5 3.9 conditional.66
  305.5 3.9 conditional.67
  314.5 3.9 conditional.68
  323.5 3.9 conditional.69
  332.5 3.9 conditional.70
  342.0 3.9 conditional.71
  347.9 4.0 collective-permute-done.35
  351.9 3.9 conditional.72
  360.9 4.0 conditional.73
  370.0 4.2 conditional.74
  382.1 3.7 copy.2312
  385.8 238.3 %reduce-scatter.4.cloned.1.call-done = f32[32,64]{1,0:T(8,128)} async-done(((f32[4096,64]{1,0:T(8,128)}), f32[32,64]{1,0:T(8,128)}) %reduce-scatter.4.cloned.1.call-update) | async-done | bytes 8208
  626.0 99.9 %psum.7 = f32[64,64]{0,1:T(8,128)S(1)} all-reduce(f32[64,64]{0,1:T(8,128)S(1)} %convolution_multiply_fusion), channel_id=1, replica_groups=mesh['src'=128,'depth'=4] {'src','depth'}, use_global_device_ids=true, to_apply=%region_79.80 | all-reduce | flops 4096 | bytes 32768 | tf_op jit(solution)/shard_map/psum | solution.py:215
  726.0 5.8 cholesky.17
  733.2 4.9 custom-call.6
  (1076 shorter events, 305.1 us)
Async XLA Ops:
  7.2 8.5 %copy-start.1 = (f32[1,4096]{1,0:T(1,128)S(1)}, f32[1,4096]{1,0:T(1,128)}, u32[]{:S(2)}) copy-start(f32[1,4096]{1,0:T(1,128)} %param.86) | copy-start | bytes 49156
  7.2 617.0 %reduce-scatter.4.cloned.1.call-start = ((), (), s32[]{:S(2)}) async-start(), calls=%async_computation.1 | async-start | bytes 2113536
  16.9 5.1 collective-permute-start
  24.7 4.2 collective-permute-start.1
  31.5 4.5 collective-permute-start.2
  44.4 2.6 collective-permute-start.3
  51.7 5.0 collective-permute-start.4
  61.3 5.0 collective-permute-start.5
  70.9 5.6 collective-permute-start.6
  81.1 5.3 collective-permute-start.7
  91.1 5.0 collective-permute-start.8
  100.7 5.0 collective-permute-start.9
  110.3 5.0 collective-permute-start.10
  119.9 5.0 collective-permute-start.11
  129.5 5.0 collective-permute-start.12
  139.1 5.0 collective-permute-start.13
  148.7 5.0 collective-permute-start.14
  158.3 5.0 collective-permute-start.15
  168.0 5.2 collective-permute-start.16
  177.7 5.5 collective-permute-start.17
  187.8 5.0 collective-permute-start.18
  193.1 9.4 %collective-permute-start.19 = (bf16[1,4,2,4096]{3,2,1,0:T(2,128)(2,1)S(1)}, bf16[1,4,2,4096]{3,2,1,0:T(2,128)(2,1)S(1)}, u32[]{:S(2)}, u32[]{:S(2)}) collective-permute-start(bf16[1,4,2,4096]{3,2,1,0:T(2,128)(2,1)S(1)} %get-tuple-element.7639), channel_id=1, source_target_pairs={{0,1},{1,2},{2,3},{4,5},{5,6},{6,7},{8,9},{9,10},{10,11},{12,13},{... | collective-permute-start | bytes 196616 | tf_op jit(solution)/shard_map/ppermute | solution.py:18
  202.6 5.0 collective-permute-start.20
  207.8 8.5 %collective-permute-start.21 = (bf16[1,4,2,4096]{3,2,1,0:T(2,128)(2,1)S(1)}, bf16[1,4,2,4096]{3,2,1,0:T(2,128)(2,1)S(1)}, u32[]{:S(2)}, u32[]{:S(2)}) collective-permute-start(bf16[1,4,2,4096]{3,2,1,0:T(2,128)(2,1)S(1)} %get-tuple-element.4124), channel_id=1, source_target_pairs={{1,0},{2,1},{3,2},{5,4},{6,5},{7,6},{9,8},{10,9},{11,10},{13,12},{... | collective-permute-start | bytes 196616 | tf_op jit(solution)/shard_map/ppermute | solution.py:18
  209.2 7.1 copy-start
  216.4 5.6 collective-permute-start.22
  222.6 19.2 %collective-permute-start.23 = (bf16[1,4,2,4096]{3,2,1,0:T(2,128)(2,1)S(1)}, bf16[1,4,2,4096]{3,2,1,0:T(2,128)(2,1)S(1)}, u32[]{:S(2)}, u32[]{:S(2)}) collective-permute-start(bf16[1,4,2,4096]{3,2,1,0:T(2,128)(2,1)S(1)} %get-tuple-element.4128), channel_id=1, source_target_pairs={{1,0},{2,1},{3,2},{5,4},{6,5},{7,6},{9,8},{10,9},{11,10},{13,12},{... | collective-permute-start | bytes 196616 | tf_op jit(solution)/shard_map/ppermute | solution.py:18
  245.8 5.0 collective-permute-start.24
  254.8 5.0 collective-permute-start.25
  263.9 5.2 collective-permute-start.26
  273.0 5.3 collective-permute-start.27
  282.4 5.0 collective-permute-start.28
  291.4 5.0 collective-permute-start.29
  300.4 5.0 collective-permute-start.30
  309.4 5.0 collective-permute-start.31
  318.4 5.0 collective-permute-start.32
  327.4 5.0 collective-permute-start.33
  336.4 5.5 collective-permute-start.34
  346.0 5.9 collective-permute-start.35
  355.9 5.0 collective-permute-start.36
  364.9 5.0 collective-permute-start.37
  374.2 5.0 collective-permute-start.38
Sparse Core Ops, SparseCore 0:
  386.0 238.1 reduce-scatter.3
where the time goes:
time: 758 us; the launch traced here: 748 us
  waiting for transfers between devices  339 us (45%)
  starting transfers between devices  104 us (14%)
  blocking collectives  99.9 us (13%)
  other arithmetic  82.9 us (11%)
  local copies, waits for them, and re-layouts  66.5 us (9%)
  matrix products  31.1 us (4%)
  between operations  18.6 us (2%)
    unnamed x2, waiting for transfers between devices  238 us
    ppermute x39, starting transfers between devices, from_behind(): return lax.ppermute(x, axis, pairs)  104 us
    ppermute x39, waiting for transfers between devices, from_behind(): return lax.ppermute(x, axis, pairs)  100 us
    psum x1, blocking collectives, shards(): gram_matrix = lax.psum(gram_local, ('src', 'depth'))  99.9 us
    another operation x16, other arithmetic, march_tangent(): jnp.stack([-scaled * background[:, None, 1], scaled * background[:, None,...  25.4 us
  transfers between devices with their start and end apart: 40, of which 39 were waited for; matrix products, arithmetic and copies ran while one was open for 2% of the time, Pallas kernels for 0%

commit v1 on v0

v1 whole, which is shorter than its diff:
```python
import math

import jax
import jax.numpy as jnp
from jax import lax
from jax.sharding import Mesh, PartitionSpec as P

SIDE = 64
CHIPS_Y = 8
CHIPS_Z = 8
CORES = 2
SRC_AXES = ("chip_y", "chip_z", "core")


DAMPING = 0.5
STEP_DEPTH = 1.0


def dft_tables(points, direction):
    counter = jnp.arange(points, dtype=jnp.int32)
    product = counter[:, None] * counter[None, :] % points
    angles = 2.0 * math.pi / points * product.astype(jnp.float32)
    cosine = jnp.cos(angles) / math.sqrt(points)
    sine_part = direction * jnp.sin(angles) / math.sqrt(points)
    matrix = jnp.stack(
        [jnp.stack([cosine, sine_part], axis=1), jnp.stack([-sine_part, cosine], axis=1)], axis=0
    )
    matrix = matrix.astype(jnp.bfloat16)
    total_points = points * points
    twist_index = counter[:, None] * counter[None, :] % total_points
    twist_angle = 2.0 * math.pi / total_points * twist_index.astype(jnp.float32)
    return (matrix, jnp.cos(twist_angle), direction * jnp.sin(twist_angle))


def transform(values, tables):
    matrix, twist_real, twist_imag = tables
    points = matrix.shape[1]
    leading = values.shape[:-2]
    grid_values = values.reshape((-1, 2 * points, points))
    square = matrix.reshape(2 * points, 2 * points)
    segmented = jnp.einsum("nkb,km->nbm", grid_values, square, preferred_element_type=jnp.float32)
    real_part = segmented[:, :, :points]
    imag_part = segmented[:, :, points:]
    turned = jnp.concatenate(
        [
            real_part * twist_real - imag_part * twist_imag,
            real_part * twist_imag + imag_part * twist_real,
        ],
        axis=-1,
    )
    turned = turned.astype(jnp.bfloat16).reshape((-1, points, 2, points))
    result = jnp.einsum("nbsc,sbtd->ntdc", turned, matrix, preferred_element_type=jnp.float32)
    return result.reshape(leading + (2, points * points))


def complex_times(first, second):
    real_part = first[..., 0, :] * second[..., 0, :] - first[..., 1, :] * second[..., 1, :]
    imag_part = first[..., 0, :] * second[..., 1, :] + first[..., 1, :] * second[..., 0, :]
    return jnp.stack([real_part, imag_part], axis=-2)


def conjugate(values):
    return jnp.stack([values[..., 0, :], -values[..., 1, :]], axis=-2)


def propagate(values, spectrum, forward, inverse):
    moved_on = transform(values.astype(jnp.bfloat16), forward)
    return transform(complex_times(moved_on, spectrum).astype(jnp.bfloat16), inverse)


def propagator(wave_nums, points_all):
    counter = jnp.arange(points_all, dtype=jnp.int32)
    folded = jnp.where(counter < points_all // 2, counter, counter - points_all).astype(jnp.float32)
    lateral = 2.0 * math.pi / points_all * folded
    excess = wave_nums[:, None] ** 2 - lateral[None, :] ** 2
    upward = jnp.sqrt(jnp.maximum(excess, 0.0)) * STEP_DEPTH
    damped = jnp.sqrt(jnp.maximum(-excess, 0.0)) * STEP_DEPTH
    real_part = jnp.where(excess > 0, jnp.cos(upward), jnp.exp(-damped))
    imag_part = jnp.where(excess > 0, jnp.sin(upward), jnp.zeros_like(upward))
    return jnp.stack([real_part, imag_part], axis=1)


def screens(wave_nums, slowness):
    phase = wave_nums[:, None, None] * STEP_DEPTH * slowness[None]
    return jnp.stack([jnp.cos(phase), jnp.sin(phase)], axis=2)


def encoded_sources(incident, encode, sources):
    shifts = jnp.arange(sources, dtype=jnp.int32)
    bit_set = encode[:, None] >> shifts[None, :] & 1
    signs_all = (1 - 2 * bit_set).astype(jnp.float32)
    return jnp.sum(signs_all[:, :, None, None] * incident, axis=1)


def lookup_waves(freq_index, wavenum, table_size):
    onehot_rows = (freq_index[:, None] == jnp.arange(table_size, dtype=jnp.int32)[None, :]).astype(
        jnp.float32
    )
    return jnp.sum(onehot_rows * wavenum[None, :], axis=1)


def shards(incident, encode, freq_index, wavenum, slowness, probes):
    points_all = SIDE * SIDE
    forward = dft_tables(SIDE, -1.0)
    inverse = dft_tables(SIDE, 1.0)
    group_count = incident.shape[0]
    probe_count = probes.shape[0]
    src_count = lax.axis_size(SRC_AXES)
    depth_count = lax.axis_size("depth")
    slowness_all = lax.all_gather(slowness, "depth", axis=0, tiled=True)
    plane_count = slowness_all.shape[0]
    probe_mine = lax.all_to_all(probes, "depth", 0, 1, tiled=True).astype(jnp.float32)
    sources = encoded_sources(incident, encode, incident.shape[1])
    wave_nums = lookup_waves(freq_index, wavenum, wavenum.shape[0])
    spectra = propagator(wave_nums, points_all)
    spectra_back = conjugate(spectra)
    plane_screens = screens(wave_nums, slowness_all)
    born_scale = wave_nums * STEP_DEPTH

    fields = []
    current = sources
    for plane in range(plane_count):
        current = complex_times(plane_screens[:, plane], propagate(current, spectra, forward, inverse))
        fields.append(current)

    def born(plane):
        scaled = born_scale[:, None, None] * probe_mine[None, :, plane]
        background = fields[plane]
        return jnp.stack([-scaled * background[:, None, 1], scaled * background[:, None, 0]], axis=2)

    tangent = born(0)
    for plane in range(1, plane_count):
        moved_on = complex_times(
            plane_screens[:, plane][:, None], propagate(tangent, spectra[:, None], forward, inverse)
        )
        tangent = moved_on + born(plane)

    adjoint = tangent
    pieces = [None] * plane_count
    for plane in reversed(range(plane_count)):
        background = fields[plane]
        product_terms = born_scale[:, None, None] * (
            background[:, None, 0] * adjoint[:, :, 1] - background[:, None, 1] * adjoint[:, :, 0]
        )
        pieces[plane] = jnp.sum(product_terms, axis=0)
        if plane > 0:
            turned_back = complex_times(conjugate(plane_screens[:, plane])[:, None], adjoint)
            adjoint = propagate(turned_back, spectra_back[:, None], forward, inverse)
    sketch_part = jnp.stack(pieces, axis=1)
    rows, planes = sketch_part.shape[0], sketch_part.shape[1]
    by_axes = sketch_part.reshape(rows, planes, CHIPS_Y, CHIPS_Z, CORES, -1)
    by_axes = jnp.transpose(by_axes, (4, 3, 2, 0, 1, 5))
    summed = lax.psum_scatter(by_axes, "core", scatter_dimension=0)
    summed = lax.psum_scatter(summed, "chip_z", scatter_dimension=0)
    summed = lax.psum_scatter(summed, "chip_y", scatter_dimension=0)
    summed = lax.all_gather(summed, "depth", axis=0, tiled=True)
    slab_width = summed.shape[2]
    src_index = lax.axis_index(SRC_AXES)
    local_probes = lax.dynamic_slice_in_dim(probes, src_index * slab_width, slab_width, 2)
    local_probes = lax.all_gather(local_probes, "depth", axis=1, tiled=True).astype(jnp.float32)
    sketch_all = summed / (group_count * src_count) + DAMPING * local_probes
    flattened_all = sketch_all.reshape(probe_count, -1)
    row_total = flattened_all.shape[1] * src_count
    gram_local = jnp.dot(flattened_all, flattened_all.T, precision=lax.Precision.HIGHEST) / row_total
    gram_matrix = lax.psum(gram_local, "core")
    gram_matrix = lax.psum(gram_matrix, "chip_z")
    gram_matrix = lax.psum(gram_matrix, "chip_y")
    sketch = lax.dynamic_slice_in_dim(sketch_all, lax.axis_index("depth"), 1, 1)
    local_planes = 1
    flattened = sketch.reshape(probe_count, local_planes * slab_width)
    lower_factor = jnp.linalg.cholesky(gram_matrix)
    identity = jnp.eye(probe_count, dtype=jnp.float32)
    inverse_lower = lax.linalg.triangular_solve(lower_factor, identity, left_side=True, lower=True)
    sketch_basis = jnp.dot(inverse_lower, flattened, precision=lax.Precision.HIGHEST).reshape(
        probe_count, local_planes, slab_width
    )
    return (sketch_basis, lower_factor.T)


def solution(mesh):
    src_size, depth_size = mesh.devices.shape
    cut = mesh.devices.reshape(CHIPS_Y, CHIPS_Z, CORES, depth_size)
    fine = Mesh(cut, SRC_AXES + ("depth",))
    in_specs = (
        P(SRC_AXES, None, None, None),
        P(SRC_AXES),
        P(SRC_AXES),
        P(),
        P("depth", None),
        P(None, "depth", None),
    )
    out_specs = (P(None, "depth", SRC_AXES), P())
    return jax.shard_map(shards, mesh=fine, in_specs=in_specs, out_specs=out_specs, check_vma=False)
```

time: 758 us -> 335 us (0.44)
  the two profiles are of different devices: /device:TPU:1 before, /device:TPU:2 now
where the time goes in v1:
time: 335 us; the launch traced here: 332 us
  blocking collectives  99.4 us (30%)
  waiting for transfers between devices  97.2 us (29%)
  local copies, waits for them, and re-layouts  49 us (15%)
  other arithmetic  46.4 us (14%)
  between operations  18.1 us (5%)
  matrix products  12 us (4%)
  starting transfers between devices  9.43 us (3%)
    reduce_scatter x1, waiting for transfers between devices, shards(): summed = lax.psum_scatter(summed, 'chip_z', scatter_dimension=0)  49.8 us
    psum x1, blocking collectives, shards(): gram_matrix = lax.psum(gram_matrix, 'chip_z')  30.9 us
    psum x1, blocking collectives, shards(): gram_matrix = lax.psum(gram_matrix, 'chip_y')  28.3 us
    reduce_scatter x1, waiting for transfers between devices, shards(): summed = lax.psum_scatter(summed, 'chip_y', scatter_dimension=0)  27.2 us
    reduce_scatter x1, waiting for transfers between devices, shards(): summed = lax.psum_scatter(by_axes, 'core', scatter_dimension=0)  20.2 us
    all_gather x1, blocking collectives, shards(): slowness_all = lax.all_gather(slowness, 'depth', axis=0, tiled=True)  12.6 us
    all_gather x1, blocking collectives, shards(): lax.all_gather(local_probes, 'depth', axis=1, tiled=True)  12.2 us
    all_gather x1, blocking collectives, shards(): summed = lax.all_gather(summed, 'depth', axis=0, tiled=True)  12 us
  transfers between devices with their start and end apart: 4, of which 3 were waited for; matrix products, arithmetic and copies ran while one was open for 9% of the time, Pallas kernels for 0%

profile of v1, /device:TPU:2, one launch (start us, length us, event | category | flops | bytes accessed | tf_op | source)
XLA Modules:
  0.0 331.6 jit_solution(9152057225294256255)
XLA Ops:
  7.7 2.0 reduce.49
  9.7 1.2 reshape.3022
  10.9 9.3 %all-to-all-start = ((bf16[4,2,32768]{2,1,0:T(2,128)(2,1)}), bf16[4,2,32768]{2,1,0:T(2,128)(2,1)S(1)}, u32[]{:S(2)}, u32[]{:S(2)}) async-start(bf16[4,2,32768]{2,1,0:T(2,128)(2,1)} %reshape.3022), calls=%async_computation | async-start | bytes 1048576 | tf_op jit(solution)/shard_map/all_to_all | solution.py:112
  21.4 1.3 fusion.124
  25.0 12.6 %all-gather.1 = f32[4,1,4096]{2,1,0:T(1,128)S(1)} all-gather(f32[1,1,4096]{2,1,0:T(1,128)} %bitcast.531), channel_id=1, replica_groups=mesh['chip_y'=8,'chip_z'=8,'core'=2,'depth'=4] {'depth'}, dimensions={0}, use_global_device_ids=true | all-gather | bytes 81920 | tf_op jit(solution)/shard_map/all_gather | solution.py:110
  37.7 2.5 cosine_bitcast_fusion
  55.3 1.2 fusion.134
  59.4 0.7 mul.2738
  60.1 0.7 mul.2528
  60.8 0.7 mul.2745
  61.6 0.7 mul.2742
  62.3 0.7 mul.2752
  63.0 0.7 mul.2749
  63.9 0.7 mul.2756
  64.9 0.7 reshape.3023
  66.3 1.7 multiply_bitcast_fusion.1
  72.0 0.8 multiply_subtract_fusion.2
  76.7 0.8 multiply_subtract_fusion.1
  81.7 0.8 subtract_convert_fusion.17
  86.7 0.9 subtract_convert_fusion.15
  91.6 0.8 subtract_convert_fusion.13
  96.4 0.9 squeeze.29
  97.3 1.9 squeeze.28
  99.2 2.1 squeeze.31
  101.3 2.8 squeeze.30
  104.1 1.9 squeeze.33
  106.0 1.9 squeeze.32
  108.0 1.8 squeeze.35
  109.8 1.9 squeeze.34
  111.8 2.3 subtract_multiply_fusion.3
  114.1 2.1 subtract_multiply_fusion.2
  116.2 0.8 subtract_multiply_fusion.1
  117.0 0.8 subtract_multiply_fusion
  117.8 2.2 maximum_bitcast_fusion
  120.1 4.4 %copy.305 = f32[2,8,8,16,4,32]{5,3,4,2,1,0:T(8,128)} copy(f32[2,8,8,16,4,32]{5,0,1,2,3,4:T(2,128)S(1)} %maximum_bitcast_fusion) | data formatting | bytes 2097152 | tf_op jit(solution)/shard_map/transpose | solution.py:152
  124.5 20.2 %reduce-scatter.4.cloned.1.call-done = f32[1,8,8,16,4,32]{5,3,4,2,1,0:T(8,128)} async-done(((f32[2,8,8,16,4,32]{5,3,4,2,1,0:T(8,128)}), f32[1,8,8,16,4,32]{5,3,4,2,1,0:T(8,128)}) %reduce-scatter.4.cloned.1.call-update) | async-done | bytes 524304 | tf_op jit(solution)/shard_map/reduce_scatter | solution.py:153
  144.8 49.8 %reduce-scatter.6.cloned.1.call-done = f32[1,8,16,4,32]{4,2,3,1,0:T(8,128)} async-done(((f32[8,8,16,4,32]{4,2,3,1,0:T(8,128)}), f32[1,8,16,4,32]{4,2,3,1,0:T(8,128)}) %reduce-scatter.6.cloned.1.call-update) | async-done | bytes 65552 | tf_op jit(solution)/shard_map/reduce_scatter | solution.py:154
  194.6 0.8 constant_dynamic-slice_fusion
  195.5 12.2 %all_gather.11 = bf16[64,4,32]{0,2,1:T(8,128)(2,1)S(1)} all-gather(bf16[64,1,32]{0,2,1:T(8,128)(2,1)S(1)} %copy.373), channel_id=1, replica_groups=mesh['chip_y'=8,'chip_z'=8,'core'=2,'depth'=4] {'depth'}, dimensions={1}, use_global_device_ids=true | all-gather | bytes 20480 | tf_op jit(solution)/shard_map/all_gather | solution.py:160
  207.7 27.2 %reduce-scatter.8.cloned.1.call-done = f32[1,16,4,32]{3,1,2,0:T(8,128)} async-done(((f32[8,16,4,32]{3,1,2,0:T(8,128)}), f32[1,16,4,32]{3,1,2,0:T(8,128)}) %reduce-scatter.8.cloned.1.call-update) | async-done | bytes 8208 | tf_op jit(solution)/shard_map/reduce_scatter | solution.py:155
  234.9 0.8 copy.306
  235.7 12.0 %all-gather = f32[1,64,4,32]{3,2,0,1:T(4,128)S(1)} all-gather(f32[1,16,4,32]{3,2,0,1:T(4,128)S(1)} %copy.306), channel_id=2, replica_groups=mesh['chip_y'=8,'chip_z'=8,'core'=2,'depth'=4] {'depth'}, dimensions={1}, use_global_device_ids=true | all-gather | bytes 40960 | tf_op jit(solution)/shard_map/all_gather | solution.py:156
  248.1 3.4 %psum.21 = f32[64,64]{0,1:T(8,128)S(1)} all-reduce(f32[64,64]{0,1:T(8,128)S(1)} %fusion), channel_id=1, replica_groups=mesh['chip_y'=8,'chip_z'=8,'core'=2,'depth'=4] {'core'}, use_global_device_ids=true, to_apply=%region_5.6 | all-reduce | flops 4096 | bytes 32768 | tf_op jit(solution)/shard_map/psum | solution.py:165
  251.5 30.9 %psum.22 = f32[64,64]{0,1:T(8,128)S(1)} all-reduce(f32[64,64]{0,1:T(8,128)S(1)} %psum.21), channel_id=1, replica_groups=mesh['chip_y'=8,'chip_z'=8,'core'=2,'depth'=4] {'chip_z'}, use_global_device_ids=true, to_apply=%region_6.7 | all-reduce | flops 4096 | bytes 32768 | tf_op jit(solution)/shard_map/psum | solution.py:166
  282.4 28.3 %psum.23 = f32[64,64]{0,1:T(8,128)S(1)} all-reduce(f32[64,64]{0,1:T(8,128)S(1)} %psum.22), channel_id=1, replica_groups=mesh['chip_y'=8,'chip_z'=8,'core'=2,'depth'=4] {'chip_y'}, use_global_device_ids=true, to_apply=%region_7.8 | all-reduce | flops 4096 | bytes 32768 | tf_op jit(solution)/shard_map/psum | solution.py:167
  310.8 5.8 %cholesky.17 = f32[64,64]{1,0:T(8,128)S(1)} custom-call(f32[64,64]{1,0:T(8,128)S(1)} %fusion.80), custom_call_target="Cholesky" | custom-call | tf_op jit(solution)/shard_map/jit(cholesky)/cholesky | solution.py:171
  318.0 4.9 %custom-call.6 = f32[1,64,64]{1,2,0:T(8,128)S(1)} custom-call(f32[1,64,64]{2,1,0:T(8,128)S(1)} %get-tuple-element.115), custom_call_target="InvertDiagBlocksLowerTriangular" | custom-call | tf_op jit(solution)/shard_map/triangular_solve | solution.py:173
  323.8 0.8 convolution_bitcast_fusion.29
  (270 shorter events, 46.7 us)
Async XLA Ops:
  7.2 34.7 %copy-start.16 = (f32[1,4,2,4096]{3,2,1,0:T(2,128)S(1)}, f32[1,4,2,4096]{3,2,1,0:T(2,128)}, u32[]{:S(2)}) copy-start(f32[1,4,2,4096]{3,2,1,0:T(2,128)} %param.6) | copy-start | bytes 393220
  10.9 54.0 %all-to-all-start = ((bf16[4,2,32768]{2,1,0:T(2,128)(2,1)}), bf16[4,2,32768]{2,1,0:T(2,128)(2,1)S(1)}, u32[]{:S(2)}, u32[]{:S(2)}) async-start(bf16[4,2,32768]{2,1,0:T(2,128)(2,1)} %reshape.3022), calls=%async_computation | async-start | bytes 1048576 | tf_op jit(solution)/shard_map/all_to_all | solution.py:112
  20.2 124.5 %reduce-scatter.4.cloned.1.call-start = ((), (), s32[]{:S(2)}) async-start(), calls=%async_computation.4 | async-start | bytes 6291456 | tf_op jit(solution)/shard_map/reduce_scatter | solution.py:153
  45.9 20.3 %copy-start.14 = (f32[1,1,4096]{2,1,0:T(1,128)}, f32[1,1,4096]{2,1,0:T(1,128)S(1)}, u32[]{:S(2)}) copy-start(f32[1,1,4096]{2,1,0:T(1,128)S(1)} %get-tuple-element.15) | copy-start | bytes 49156
  46.0 20.3 %copy-start.15 = (f32[1,1,4096]{2,1,0:T(1,128)}, f32[1,1,4096]{2,1,0:T(1,128)S(1)}, u32[]{:S(2)}) copy-start(f32[1,1,4096]{2,1,0:T(1,128)S(1)} %get-tuple-element.111) | copy-start | bytes 49156
  49.3 17.0 %copy-start.10 = (f32[1,1,4096]{2,1,0:T(1,128)}, f32[1,1,4096]{2,1,0:T(1,128)S(1)}, u32[]{:S(2)}) copy-start(f32[1,1,4096]{2,1,0:T(1,128)S(1)} %get-tuple-element.19) | copy-start | bytes 49156
  49.3 17.0 %copy-start.11 = (f32[1,1,4096]{2,1,0:T(1,128)}, f32[1,1,4096]{2,1,0:T(1,128)S(1)}, u32[]{:S(2)}) copy-start(f32[1,1,4096]{2,1,0:T(1,128)S(1)} %get-tuple-element.107) | copy-start | bytes 49156
  52.6 13.7 %copy-start.12 = (f32[1,1,4096]{2,1,0:T(1,128)}, f32[1,1,4096]{2,1,0:T(1,128)S(1)}, u32[]{:S(2)}) copy-start(f32[1,1,4096]{2,1,0:T(1,128)S(1)} %get-tuple-element.23) | copy-start | bytes 49156
  52.6 13.7 %copy-start.13 = (f32[1,1,4096]{2,1,0:T(1,128)}, f32[1,1,4096]{2,1,0:T(1,128)S(1)}, u32[]{:S(2)}) copy-start(f32[1,1,4096]{2,1,0:T(1,128)S(1)} %get-tuple-element.105) | copy-start | bytes 49156
  79.5 2.1 copy-start.17
  79.5 2.1 copy-start.18
  80.3 1.5 copy-start.23
  80.3 1.5 copy-start.24
  82.5 2.1 copy-start.9
  84.7 2.0 copy-start.21
  84.7 2.0 copy-start.22
  89.5 2.0 copy-start.19
  89.5 2.0 copy-start.20
  96.4 7.8 %copy-start.4 = (f32[1,16,1,4096]{3,1,2,0:T(8,128)S(1)}, f32[1,16,1,4096]{3,1,2,0:T(8,128)}, u32[]{:S(2)}) copy-start(f32[1,16,1,4096]{3,1,2,0:T(8,128)} %get-tuple-element.89) | copy-start | bytes 786436
  96.4 9.7 %copy-start.3 = (f32[1,16,1,4096]{3,1,2,0:T(8,128)S(1)}, f32[1,16,1,4096]{3,1,2,0:T(8,128)}, u32[]{:S(2)}) copy-start(f32[1,16,1,4096]{3,1,2,0:T(8,128)} %get-tuple-element.88) | copy-start | bytes 786436
  99.2 12.5 %copy-start.5 = (f32[8,8,2,32]{3,2,1,0:T(2,128)S(1)}, f32[8,8,2,32]{3,2,1,0:T(2,128)}, u32[]{:S(2)}) copy-start(f32[8,8,2,32]{3,2,1,0:T(2,128)} %mul.2738) | copy-start | bytes 49156
  111.7 4.4 %copy-start = (f32[16,1,8,8,2,32]{5,4,3,2,0,1:T(2,128)S(1)}, f32[16,1,8,8,2,32]{5,4,3,2,0,1:T(2,128)}, u32[]{:S(2)}) copy-start(f32[16,1,8,8,2,32]{5,4,3,2,0,1:T(2,128)} %squeeze.33) | copy-start | bytes 786436
  111.7 4.5 %copy-start.2 = (f32[16,1,8,8,2,32]{5,4,3,2,0,1:T(2,128)S(1)}, f32[16,1,8,8,2,32]{5,4,3,2,0,1:T(2,128)}, u32[]{:S(2)}) copy-start(f32[16,1,8,8,2,32]{5,4,3,2,0,1:T(2,128)} %squeeze.32) | copy-start | bytes 786436
  111.7 4.5 %copy-start.6 = (f32[8,8,2,32]{3,2,1,0:T(2,128)S(1)}, f32[8,8,2,32]{3,2,1,0:T(2,128)}, u32[]{:S(2)}) copy-start(f32[8,8,2,32]{3,2,1,0:T(2,128)} %mul.2752) | copy-start | bytes 49156
  111.7 4.5 %copy-start.8 = (f32[8,8,2,32]{3,2,1,0:T(2,128)S(1)}, f32[8,8,2,32]{3,2,1,0:T(2,128)}, u32[]{:S(2)}) copy-start(f32[8,8,2,32]{3,2,1,0:T(2,128)} %mul.2749) | copy-start | bytes 49156
  111.7 5.3 %copy-start.1 = (f32[16,1,8,8,2,32]{5,4,3,2,0,1:T(2,128)S(1)}, f32[16,1,8,8,2,32]{5,4,3,2,0,1:T(2,128)}, u32[]{:S(2)}) copy-start(f32[16,1,8,8,2,32]{5,4,3,2,0,1:T(2,128)} %squeeze.34) | copy-start | bytes 786436
  111.7 5.3 %copy-start.7 = (f32[8,8,2,32]{3,2,1,0:T(2,128)S(1)}, f32[8,8,2,32]{3,2,1,0:T(2,128)}, u32[]{:S(2)}) copy-start(f32[8,8,2,32]{3,2,1,0:T(2,128)} %mul.2756) | copy-start | bytes 49156
  124.5 70.1 %reduce-scatter.6.cloned.1.call-start = ((), (), s32[]{:S(2)}) async-start(), calls=%async_computation.5 | async-start | bytes 2359296 | tf_op jit(solution)/shard_map/reduce_scatter | solution.py:154
  144.7 90.2 %reduce-scatter.8.cloned.1.call-start = ((), (), s32[]{:S(2)}) async-start(), calls=%async_computation.6 | async-start | bytes 294912 | tf_op jit(solution)/shard_map/reduce_scatter | solution.py:155
Sparse Core Ops, SparseCore 0:
  124.6 20.0 reduce-scatter.3
  147.8 46.7 reduce-scatter.5
  197.6 37.2 reduce-scatter.7

commit v2 on v1

--- a/solution.py
+++ b/solution.py
@@ -3,6 +3,8 @@
 import jax
 import jax.numpy as jnp
 from jax import lax
+from jax.experimental import pallas as pl
+from jax.experimental.pallas import tpu as pltpu
 from jax.sharding import Mesh, PartitionSpec as P
 
 SIDE = 64
@@ -99,6 +101,79 @@
     return jnp.sum(onehot_rows * wavenum[None, :], axis=1)
 
 
+def gram_sum_kernel(stages, part_ref, out_ref, *scratch):
+    count = len(stages)
+    slots = scratch[:count]
+    send_sems, recv_sems, carried = scratch[count], scratch[count + 1], scratch[count + 2]
+    barrier = pltpu.get_barrier_semaphore()
+    peers_total = 0
+    for axis, size in stages:
+        me = lax.axis_index(axis)
+        for step in range(1, size):
+            pl.semaphore_signal(barrier, inc=1, device_id={axis: lax.rem(me + step, size)},
+                                device_id_type=pl.DeviceIdType.MESH)
+            peers_total += 1
+    pl.semaphore_wait(barrier, peers_total)
+    carried[...] = part_ref[...]
+    used = 0
+    offset = 0
+    for stage, (axis, size) in enumerate(stages):
+        me = lax.axis_index(axis)
+        slot = slots[stage]
+        copies = []
+        for step in range(1, size):
+            copy = pltpu.make_async_remote_copy(
+                src_ref=carried,
+                dst_ref=slot.at[me],
+                send_sem=send_sems.at[used + step - 1],
+                recv_sem=recv_sems.at[offset + me],
+                device_id={axis: lax.rem(me + step, size)},
+                device_id_type=pl.DeviceIdType.MESH,
+            )
+            copy.start()
+            copies.append(copy)
+        slot[me] = carried[...]
+        for copy in copies:
+            copy.wait_send()
+        for step in range(1, size):
+            sender = lax.rem(me + size - step, size)
+            incoming = pltpu.make_async_remote_copy(
+                src_ref=carried,
+                dst_ref=slot.at[sender],
+                send_sem=send_sems.at[used + step - 1],
+                recv_sem=recv_sems.at[offset + sender],
+                device_id={axis: lax.rem(me + step, size)},
+                device_id_type=pl.DeviceIdType.MESH,
+            )
+            incoming.wait_recv()
+        used += size - 1
+        offset += size
+        total = slot[0]
+        for member in range(1, size):
+            total = total + slot[member]
+        carried[...] = total
+    out_ref[...] = carried[...]
+
+
+def gram_sum(part, stages):
+    stages = [(axis, size) for axis, size in stages if size > 1]
+    sends = sum(size - 1 for _, size in stages)
+    scratch = [pltpu.VMEM((size,) + part.shape, jnp.float32) for _, size in stages]
+    scratch += [
+        pltpu.SemaphoreType.DMA((max(sends, 1),)),
+        pltpu.SemaphoreType.DMA((max(sum(size for _, size in stages), 1),)),
+        pltpu.VMEM(part.shape, jnp.float32),
+    ]
+    return pl.pallas_call(
+        lambda *refs: gram_sum_kernel(stages, *refs),
+        out_shape=jax.ShapeDtypeStruct(part.shape, jnp.float32),
+        in_specs=[pl.BlockSpec(memory_space=pltpu.VMEM)],
+        out_specs=pl.BlockSpec(memory_space=pltpu.VMEM),
+        scratch_shapes=scratch,
+        compiler_params=pltpu.CompilerParams(collective_id=0, has_side_effects=True),
+    )(part)
+
+
 def shards(incident, encode, freq_index, wavenum, slowness, probes):
     points_all = SIDE * SIDE
     forward = dft_tables(SIDE, -1.0)
@@ -107,7 +182,8 @@
     probe_count = probes.shape[0]
     src_count = lax.axis_size(SRC_AXES)
     depth_count = lax.axis_size("depth")
-    slowness_all = lax.all_gather(slowness, "depth", axis=0, tiled=True)
+    spread = jnp.broadcast_to(slowness[None], (depth_count,) + slowness.shape)
+    slowness_all = lax.all_to_all(spread, "depth", 0, 0, tiled=True).reshape(-1, slowness.shape[-1])
     plane_count = slowness_all.shape[0]
     probe_mine = lax.all_to_all(probes, "depth", 0, 1, tiled=True).astype(jnp.float32)
     sources = encoded_sources(incident, encode, incident.shape[1])
@@ -153,18 +229,20 @@
     summed = lax.psum_scatter(by_axes, "core", scatter_dimension=0)
     summed = lax.psum_scatter(summed, "chip_z", scatter_dimension=0)
     summed = lax.psum_scatter(summed, "chip_y", scatter_dimension=0)
-    summed = lax.all_gather(summed, "depth", axis=0, tiled=True)
-    slab_width = summed.shape[2]
+    slab_width = summed.shape[-1]
     src_index = lax.axis_index(SRC_AXES)
-    local_probes = lax.dynamic_slice_in_dim(probes, src_index * slab_width, slab_width, 2)
-    local_probes = lax.all_gather(local_probes, "depth", axis=1, tiled=True).astype(jnp.float32)
+    probe_slab = lax.dynamic_slice_in_dim(probes, src_index * slab_width, slab_width, 2)
+    probe_slab = jnp.transpose(probe_slab.reshape(depth_count, rows, slab_width), (1, 0, 2))
+    both = jnp.stack([summed.reshape(rows, planes, slab_width), probe_slab.astype(jnp.float32)])
+    both = lax.all_gather(both, "depth", axis=0)
+    summed = both[:, 0].reshape(probe_count, planes, slab_width)
+    local_probes = jnp.transpose(both[:, 1], (2, 1, 0, 3)).reshape(probe_count, planes, slab_width)
     sketch_all = summed / (group_count * src_count) + DAMPING * local_probes
     flattened_all = sketch_all.reshape(probe_count, -1)
     row_total = flattened_all.shape[1] * src_count
     gram_local = jnp.dot(flattened_all, flattened_all.T, precision=lax.Precision.HIGHEST) / row_total
-    gram_matrix = lax.psum(gram_local, "core")
-    gram_matrix = lax.psum(gram_matrix, "chip_z")
-    gram_matrix = lax.psum(gram_matrix, "chip_y")
+    stage_sizes = [(axis, lax.axis_size(axis)) for axis in ("core", "chip_z", "chip_y")]
+    gram_matrix = gram_sum(gram_local, stage_sizes)
     sketch = lax.dynamic_slice_in_dim(sketch_all, lax.axis_index("depth"), 1, 1)
     local_planes = 1
     flattened = sketch.reshape(probe_count, local_planes * slab_width)

time: 335 us -> 298 us (0.89)
  the two profiles are of different devices: /device:TPU:2 before, /device:TPU:1 now
where the time goes in v2:
time: 298 us; the launch traced here: 293 us
  waiting for transfers between devices  110 us (37%)
  local copies, waits for them, and re-layouts  50 us (17%)
  other arithmetic  48.2 us (16%)
  Pallas kernels  34.5 us (12%)
  between operations  18.1 us (6%)
  matrix products  12.7 us (4%)
  starting transfers between devices  9.68 us (3%)
  blocking collectives  9.65 us (3%)
    reduce_scatter x1, waiting for transfers between devices, shards(): summed = lax.psum_scatter(summed, 'chip_z', scatter_dimension=0)  43.7 us
    reduce_scatter x1, waiting for transfers between devices, shards(): summed = lax.psum_scatter(summed, 'chip_y', scatter_dimension=0)  38.9 us
    pallas_call x1, Pallas kernels, gram_sum(): pl.pallas_call(lambda *refs: gram_sum_kernel(stages, *refs), out_shape=ja...  34.5 us
    reduce_scatter x1, waiting for transfers between devices, shards(): summed = lax.psum_scatter(by_axes, 'core', scatter_dimension=0)  27.6 us
    all_gather x1, blocking collectives, shards(): both = lax.all_gather(both, 'depth', axis=0)  9.65 us
    another operation x30, other arithmetic  7.22 us
    mul x4, other arithmetic, shards(): born_scale[:, None, None]  6.9 us
    squeeze x3, local copies, waits for them, and re-layouts, complex_times(): second[..., 1, :]  6.62 us
  transfers between devices with their start and end apart: 5, of which 3 were waited for; matrix products, arithmetic and copies ran while one was open for 12% of the time, Pallas kernels for 0%

profile of v2, /device:TPU:1, one launch (start us, length us, event | category | flops | bytes accessed | tf_op | source)
XLA Modules:
  0.0 293.1 jit_solution(9150131505357925370)
XLA Ops:
  7.2 1.4 broadcast_in_dim.16
  8.5 4.8 %all-to-all-start = ((f32[4,1,4096]{2,1,0:T(1,128)}), f32[4,1,4096]{2,1,0:T(1,128)S(1)}, u32[]{:S(2)}, u32[]{:S(2)}) async-start(f32[4,1,4096]{2,1,0:T(1,128)} %broadcast_in_dim.16), calls=%async_computation | async-start | bytes 131072 | tf_op jit(solution)/shard_map/all_to_all | solution.py:186
  14.6 1.3 fusion.126
  19.2 1.0 multiply_reduce_fusion
  24.0 2.0 reduce.49
  26.0 1.2 reshape.3059
  27.2 4.2 %all-to-all-start.1 = ((bf16[4,2,32768]{2,1,0:T(2,128)(2,1)}), bf16[4,2,32768]{2,1,0:T(2,128)(2,1)S(1)}, u32[]{:S(2)}, u32[]{:S(2)}) async-start(bf16[4,2,32768]{2,1,0:T(2,128)(2,1)} %reshape.3059), calls=%async_computation.1 | async-start | bytes 1048576 | tf_op jit(solution)/shard_map/all_to_all | solution.py:188
  32.0 2.5 cosine_bitcast_fusion
  45.6 1.2 fusion.135
  48.8 0.7 mul.2768
  49.6 0.7 mul.2558
  50.3 0.7 mul.2775
  51.0 0.7 mul.2772
  51.7 0.7 mul.2782
  52.5 0.7 mul.2779
  53.2 0.7 mul.2789
  53.9 0.7 mul.2786
  56.0 1.6 multiply_bitcast_fusion.1
  70.0 0.8 subtract_convert_fusion.17
  75.0 0.9 subtract_convert_fusion.15
  79.8 0.9 subtract_convert_fusion.13
  84.7 0.9 squeeze.29
  85.6 1.9 squeeze.28
  87.5 2.1 squeeze.31
  89.6 2.9 squeeze.30
  92.5 1.9 squeeze.33
  94.4 1.9 squeeze.32
  96.3 1.8 squeeze.35
  98.1 1.9 squeeze.34
  100.0 2.4 subtract_multiply_fusion.3
  102.4 2.1 subtract_multiply_fusion.2
  104.5 1.7 subtract_multiply_fusion.1
  106.2 0.8 subtract_multiply_fusion
  107.0 2.2 maximum_bitcast_fusion
  109.2 4.4 %copy.416 = f32[2,8,8,16,4,32]{5,3,4,2,1,0:T(8,128)} copy(f32[2,8,8,16,4,32]{5,0,1,2,3,4:T(2,128)S(1)} %maximum_bitcast_fusion) | data formatting | bytes 2097152 | tf_op jit(solution)/shard_map/transpose | solution.py:228
  113.7 27.6 %reduce-scatter.4.cloned.1.call-done = f32[1,8,8,16,4,32]{5,3,4,2,1,0:T(8,128)} async-done(((f32[2,8,8,16,4,32]{5,3,4,2,1,0:T(8,128)}), f32[1,8,8,16,4,32]{5,3,4,2,1,0:T(8,128)}) %reduce-scatter.4.cloned.1.call-update) | async-done | bytes 524304 | tf_op jit(solution)/shard_map/reduce_scatter | solution.py:229
  141.4 0.8 constant_dynamic-slice_fusion
  142.2 43.7 %reduce-scatter.6.cloned.1.call-done = f32[1,8,16,4,32]{4,2,3,1,0:T(8,128)} async-done(((f32[8,8,16,4,32]{4,2,3,1,0:T(8,128)}), f32[1,8,16,4,32]{4,2,3,1,0:T(8,128)}) %reduce-scatter.6.cloned.1.call-update) | async-done | bytes 65552 | tf_op jit(solution)/shard_map/reduce_scatter | solution.py:230
  185.9 38.9 %reduce-scatter.8.cloned.1.call-done = f32[1,16,4,32]{3,1,2,0:T(8,128)} async-done(((f32[8,16,4,32]{3,1,2,0:T(8,128)}), f32[1,16,4,32]{3,1,2,0:T(8,128)}) %reduce-scatter.8.cloned.1.call-update) | async-done | bytes 8208 | tf_op jit(solution)/shard_map/reduce_scatter | solution.py:231
  224.8 0.8 pad_maximum_fusion.24
  225.5 9.6 %all-gather = f32[8,16,4,32]{3,1,2,0:T(8,128)S(1)} all-gather(f32[2,16,4,32]{3,1,2,0:T(8,128)S(1)} %pad_maximum_fusion.24), channel_id=2, replica_groups=mesh['chip_y'=8,'chip_z'=8,'core'=2,'depth'=4] {'depth'}, dimensions={0}, use_global_device_ids=true | all-gather | bytes 81920 | tf_op jit(solution)/shard_map/all_gather | solution.py:237
  235.2 0.9 fusion.refs_0_
  236.1 34.5 %shard_map.77 = f32[64,64]{1,0:T(8,128)} custom-call(f32[64,64]{1,0:T(8,128)} %fusion.refs_0_), custom_call_target="tpu_custom_call" | custom-call | tf_op jit(solution)/shard_map/pallas_call | solution.py:167
  270.6 0.8 copy.420
  271.5 0.8 fusion.83
  272.3 5.8 %cholesky.17 = f32[64,64]{1,0:T(8,128)S(1)} custom-call(f32[64,64]{1,0:T(8,128)S(1)} %fusion.83), custom_call_target="Cholesky" | custom-call | tf_op jit(solution)/shard_map/jit(cholesky)/cholesky | solution.py:249
  279.4 4.9 %custom-call.6 = f32[1,64,64]{1,2,0:T(8,128)S(1)} custom-call(f32[1,64,64]{2,1,0:T(8,128)S(1)} %get-tuple-element.121), custom_call_target="InvertDiagBlocksLowerTriangular" | custom-call | tf_op jit(solution)/shard_map/triangular_solve | solution.py:251
  285.3 0.8 convolution_bitcast_fusion.29
  (263 shorter events, 46.6 us)
Async XLA Ops:
  8.5 18.7 %all-to-all-start = ((f32[4,1,4096]{2,1,0:T(1,128)}), f32[4,1,4096]{2,1,0:T(1,128)S(1)}, u32[]{:S(2)}, u32[]{:S(2)}) async-start(f32[4,1,4096]{2,1,0:T(1,128)} %broadcast_in_dim.16), calls=%async_computation | async-start | bytes 131072 | tf_op jit(solution)/shard_map/all_to_all | solution.py:186
  27.2 27.4 %all-to-all-start.1 = ((bf16[4,2,32768]{2,1,0:T(2,128)(2,1)}), bf16[4,2,32768]{2,1,0:T(2,128)(2,1)S(1)}, u32[]{:S(2)}, u32[]{:S(2)}) async-start(bf16[4,2,32768]{2,1,0:T(2,128)(2,1)} %reshape.3059), calls=%async_computation.1 | async-start | bytes 1048576 | tf_op jit(solution)/shard_map/all_to_all | solution.py:188
  31.5 109.9 %reduce-scatter.4.cloned.1.call-start = ((), (), s32[]{:S(2)}) async-start(), calls=%async_computation.5 | async-start | bytes 6291456 | tf_op jit(solution)/shard_map/reduce_scatter | solution.py:229
  36.4 19.6 %copy-start.8 = (f32[1,1,4096]{2,1,0:T(1,128)}, f32[1,1,4096]{2,1,0:T(1,128)S(1)}, u32[]{:S(2)}) copy-start(f32[1,1,4096]{2,1,0:T(1,128)S(1)} %get-tuple-element.17) | copy-start | bytes 49156
  36.4 19.6 %copy-start.9 = (f32[1,1,4096]{2,1,0:T(1,128)}, f32[1,1,4096]{2,1,0:T(1,128)S(1)}, u32[]{:S(2)}) copy-start(f32[1,1,4096]{2,1,0:T(1,128)S(1)} %get-tuple-element.117) | copy-start | bytes 49156
  43.0 13.0 %copy-start.7 = (f32[1,1,4096]{2,1,0:T(1,128)}, f32[1,1,4096]{2,1,0:T(1,128)S(1)}, u32[]{:S(2)}) copy-start(f32[1,1,4096]{2,1,0:T(1,128)S(1)} %get-tuple-element.111) | copy-start | bytes 49156
  59.6 2.0 copy-start.14
  59.6 2.0 copy-start.15
  63.7 2.0 copy-start.12
  63.7 2.0 copy-start.13
  67.8 2.1 copy-start.10
  67.8 2.1 copy-start.11
  68.5 1.4 copy-start.20
  68.6 1.4 copy-start.21
  72.9 2.0 copy-start.18
  72.9 2.0 copy-start.19
  77.8 2.0 copy-start.16
  77.8 2.0 copy-start.17
  84.7 7.8 %copy-start.4 = (f32[1,16,1,4096]{3,1,2,0:T(8,128)S(1)}, f32[1,16,1,4096]{3,1,2,0:T(8,128)}, u32[]{:S(2)}) copy-start(f32[1,16,1,4096]{3,1,2,0:T(8,128)} %get-tuple-element.91) | copy-start | bytes 786436
  84.7 9.7 %copy-start.3 = (f32[1,16,1,4096]{3,1,2,0:T(8,128)S(1)}, f32[1,16,1,4096]{3,1,2,0:T(8,128)}, u32[]{:S(2)}) copy-start(f32[1,16,1,4096]{3,1,2,0:T(8,128)} %get-tuple-element.90) | copy-start | bytes 786436
  100.0 4.5 %copy-start = (f32[16,1,8,8,2,32]{5,4,3,2,0,1:T(2,128)S(1)}, f32[16,1,8,8,2,32]{5,4,3,2,0,1:T(2,128)}, u32[]{:S(2)}) copy-start(f32[16,1,8,8,2,32]{5,4,3,2,0,1:T(2,128)} %squeeze.33) | copy-start | bytes 786436
  100.0 4.5 %copy-start.2 = (f32[16,1,8,8,2,32]{5,4,3,2,0,1:T(2,128)S(1)}, f32[16,1,8,8,2,32]{5,4,3,2,0,1:T(2,128)}, u32[]{:S(2)}) copy-start(f32[16,1,8,8,2,32]{5,4,3,2,0,1:T(2,128)} %squeeze.32) | copy-start | bytes 786436
  100.0 6.2 %copy-start.1 = (f32[16,1,8,8,2,32]{5,4,3,2,0,1:T(2,128)S(1)}, f32[16,1,8,8,2,32]{5,4,3,2,0,1:T(2,128)}, u32[]{:S(2)}) copy-start(f32[16,1,8,8,2,32]{5,4,3,2,0,1:T(2,128)} %squeeze.34) | copy-start | bytes 786436
  100.0 6.2 %copy-start.5 = (f32[8,8,2,32]{3,2,1,0:T(2,128)S(1)}, f32[8,8,2,32]{3,2,1,0:T(2,128)}, u32[]{:S(2)}) copy-start(f32[8,8,2,32]{3,2,1,0:T(2,128)} %mul.2789) | copy-start | bytes 49156
  100.0 6.2 %copy-start.6 = (f32[8,8,2,32]{3,2,1,0:T(2,128)S(1)}, f32[8,8,2,32]{3,2,1,0:T(2,128)}, u32[]{:S(2)}) copy-start(f32[8,8,2,32]{3,2,1,0:T(2,128)} %mul.2786) | copy-start | bytes 49156
  113.6 72.2 %reduce-scatter.6.cloned.1.call-start = ((), (), s32[]{:S(2)}) async-start(), calls=%async_computation.6 | async-start | bytes 2359296 | tf_op jit(solution)/shard_map/reduce_scatter | solution.py:230
  141.3 83.4 %reduce-scatter.8.cloned.1.call-start = ((), (), s32[]{:S(2)}) async-start(), calls=%async_computation.7 | async-start | bytes 294912 | tf_op jit(solution)/shard_map/reduce_scatter | solution.py:231
Sparse Core Ops, SparseCore 0:
  113.8 27.5 reduce-scatter.3
  144.4 41.4 reduce-scatter.5
  188.9 35.8 reduce-scatter.7
